TPU v7x, 128 devices: a whole 4x4x4 slice. The times are simulated.
128 devices in a mesh: fit: 8 (over x, core), ao: 16 (over z, y).
Axes of the slice: x: 4, y: 4, z: 4, core: 2. Of those that a mesh axis runs over, the one named last changes fastest.
Arguments:
- three_index: bfloat16 [64, 128, 128, 1024], P('ao', None, None, 'fit'), may hold values from -384 to 384
- occ_coeff: bfloat16 [128, 128, 128], P(('fit', 'ao')), may hold values from -0.005859375 to 0.005859375
- occ_owner: int32 [2], replicated, may hold values from 0 to 127
- screen: int32 [64, 8], P('ao', 'fit'), may hold values 0 or 1
- tile_owner: int32 [2048, 1], P(('fit', 'ao')), may hold values from 0 to 15; in each aligned block of 16 rows (0 to 15, 16 to 31, ...) at most 2 rows name the same one
- tile_slot: int32 [2048], P(('fit', 'ao')), may hold values from 0 to 15
Outputs:
- fock: float32 [256, 128, 128], P(('fit', 'ao'))
Inputs may be any that keep to these rules, and one draw needn't show every extreme that they name: `tile_owner`: among the 16 tiles of one device, at most 2 name the same owner; some device sends exactly 2 tiles to some owner.
All inputs are finite; a program needn't handle non-finite values. No bound on the sum of `screen` on one device may be relied on, other than what follows from the above.
Results may differ from a plain program's by a relative error of at most 0.0003.
Values may be sent and summed in bfloat16 or wider, within the bound.
A program may use at most 192 MiB of HBM per device.

v0:
```python
import jax
import jax.numpy as jnp
from jax import lax
from jax.sharding import PartitionSpec as P

FT_DEV = 2


def spread(value, axis, source):
    kept = jnp.where(lax.axis_index(axis) == source, value, 0).astype(value.dtype)
    return lax.psum(kept, axis)


def on_device(three_index, occ_coeff, occ_owner, screen, tile_owner, tile_slot):
    blocks = []
    for which in range(2):
        blocks.append(spread(occ_coeff[0], ("fit", "ao"), occ_owner[which]))
    coeff = jnp.concatenate(blocks, axis=1)
    mub = three_index.shape[0]
    width = three_index.shape[2]
    half = jnp.einsum("jvmp,vi->jmpi", three_index, coeff, preferred_element_type=jnp.float32)
    half = (half * screen[:, 0].astype(jnp.float32)[:, None, None, None]).astype(jnp.bfloat16)
    flat = half.reshape(mub, width, -1)
    gram = jnp.einsum("jmx,knx->jkmn", flat, flat, preferred_element_type=jnp.float32)
    gram = gram.reshape(mub * mub, width * width)
    owners = tile_owner[:, 0]
    n_ao = lax.axis_size("ao")
    n_fit = lax.axis_size("fit")
    total_slots = FT_DEV * n_fit
    glob = tile_slot // FT_DEV * (n_ao * FT_DEV) + owners * FT_DEV + tile_slot % FT_DEV
    table = (jnp.arange(n_ao * total_slots, dtype=jnp.int32)[:, None] == glob[None, :]).astype(
        jnp.float32
    )
    dense = jnp.dot(table, gram, precision=lax.Precision.HIGHEST).reshape(
        n_ao * total_slots, width, width
    )
    fock = lax.psum_scatter(dense, ("fit", "ao"), scatter_dimension=0, tiled=True)
    return fock


def solution(mesh):
    in_specs = (
        P("ao", None, None, "fit"),
        P(("fit", "ao"), None, None),
        P(),
        P("ao", "fit"),
        P(("fit", "ao"), None),
        P(("fit", "ao")),
    )
    out_specs = P(("fit", "ao"), None, None)
    return jax.shard_map(
        on_device, mesh=mesh, in_specs=in_specs, out_specs=out_specs, check_vma=False
    )
```

profile of v0, /device:TPU:0, one launch (start us, length us, event | category | flops | bytes accessed | tf_op | source)
XLA Modules:
  0.0 900.0 jit_solution(17139120014047330572)
XLA Ops:
  6.5 0.0 all-reduce.3.cloned.1.call-start
  6.5 1.3 fusion.18
  9.1 0.9 copy.11
  10.0 0.6 select_bitcast_fusion.1
  10.6 0.0 all-reduce.3.cloned.1.call-update
  10.7 0.0 reduce-scatter.2.cloned.1.call-start
  10.7 0.7 fusion.16
  11.4 0.7 convert_bitcast_fusion
  12.1 23.6 %copy.13 = bf16[4,128,128,128]{2,1,3,0:T(8,128)(2,1)} copy(bf16[4,128,128,128]{3,2,1,0:T(8,128)(2,1)} %param.6) | data formatting | bytes 33554432 | tf_op args[0]
  35.7 114.9 %all-reduce.3.cloned.1.call-done = (bf16[128,128]{0,1:T(8,128)(2,1)}, bf16[128,128]{0,1:T(8,128)(2,1)}) async-done(((bf16[128,128]{0,1:T(8,128)(2,1)}, bf16[128,128]{0,1:T(8,128)(2,1)}), (bf16[128,128]{0,1:T(8,128)(2,1)}, bf16[128,128]{0,1:T(8,128)(2,1)})) %all-reduce.3.cloned.1.call-update) | async-done | bytes 65552 | tf_op jit(solution)/shard_map/psum | solution.py:11
  150.6 19.5 %multiply_convert_fusion = bf16[256,4,128,128]{2,0,3,1:T(8,128)(2,1)} fusion(bf16[4,128,128,128]{2,1,3,0:T(8,128)(2,1)} %copy.13, f32[4]{0:T(128)S(1)} %convert_bitcast_fusion, bf16[128,128]{0,1:T(8,128)(2,1)} %get-tuple-element.5, bf16[128,128]{0,1:T(8,128)(2,1)} %get-tuple-element.6), kind=kOutput, calls=%fused_computation | convolution fusion | flops 4328652800 | bytes 50397200 | tf_op jit(solution)/shard_map/jvmp,vi->jmpi/dot_general | solution.py:21
  170.1 27.5 %fusion.3 = f32[4,4,128,128]{2,3,0,1:T(8,128)S(1)} fusion(bf16[256,4,128,128]{2,0,3,1:T(8,128)(2,1)} %multiply_convert_fusion), kind=kOutput, calls=%fused_computation.4 | convolution fusion | flops 17179869184 | bytes 34603008 | tf_op jit(solution)/shard_map/jmx,knx->jkmn/dot_general | solution.py:24
  197.6 0.3 copy.16
  197.9 6.8 fusion.8
  204.7 20.0 %copy.18 = f32[256,128,128]{2,1,0:T(8,128)} copy(f32[256,128,128]{2,0,1:T(8,128)S(1)} %fusion.8) | data formatting | bytes 33554432 | tf_op jit(solution)/shard_map/dot_general | solution.py:34
  224.8 0.0 reduce-scatter.2.cloned.1.call-update
  224.8 668.4 %reduce-scatter.2.cloned.1.call-done = f32[2,128,128]{2,1,0:T(8,128)} async-done(((f32[256,128,128]{2,1,0:T(8,128)}), f32[2,128,128]{2,1,0:T(8,128)}) %reduce-scatter.2.cloned.1.call-update) | async-done | bytes 131088 | tf_op jit(solution)/shard_map/reduce_scatter | solution.py:37
Async XLA Ops:
  6.5 144.1 %all-reduce.3.cloned.1.call-start = ((), (), s32[]{:S(2)}) async-start(), calls=%async_computation.2 | async-start | bytes 131072 | tf_op jit(solution)/shard_map/psum | solution.py:11
  10.7 882.5 %reduce-scatter.2.cloned.1.call-start = ((), (), s32[]{:S(2)}) async-start(), calls=%async_computation.1 | async-start | bytes 16908288 | tf_op jit(solution)/shard_map/reduce_scatter | solution.py:37
Sparse Core Ops, SparseCore 0:
  12.4 138.1 all-reduce.2
  224.9 668.1 reduce-scatter.1
where the time goes:
time: 901 us; the launch traced here: 900 us
  waiting for transfers between devices  783 us (87%)
  matrix products  53.8 us (6%)
  local copies, waits for them, and re-layouts  46.2 us (5%)
  between operations  14.7 us (2%)
    reduce_scatter x1, waiting for transfers between devices, on_device(): lax.psum_scatter(dense, ('fit', 'ao'), scatter_dimension=0, tiled=True)  668 us
    psum x1, waiting for transfers between devices, spread(): return lax.psum(kept, axis)  115 us
    dot_general x1, matrix products, on_device(): jnp.einsum('jmx,knx->jkmn', flat, flat, preferred_element_type=jnp.float32)  27.5 us
    unnamed x2, local copies, waits for them, and re-layouts  24.5 us
    dot_general x1, local copies, waits for them, and re-layouts, on_device(): jnp.dot(table, gram, precision=lax.Precision.HIGHEST)  20 us
    dot_general x1, matrix products, on_device(): jnp.einsum('jvmp,vi->jmpi', three_index, coeff, preferred_element_type=jn...  19.5 us
  transfers between devices with their start and end apart: 2, of which 2 were waited for; matrix products, arithmetic and copies ran while one was open for 3% of the time, Pallas kernels for 0%

commit v1 on v0

v1 whole, which is shorter than its diff:
```python
import functools

import jax
import jax.numpy as jnp
from jax import lax
from jax.experimental import pallas as pl
from jax.experimental.pallas import tpu as pltpu
from jax.sharding import PartitionSpec as P

MESH = pl.DeviceIdType.MESH
NF = 8
NA = 16
SIDE = 4
CAP = 2
SLOTS = 16
W = 128
CHUNKS = 4
ROWS = W // CHUNKS


def ao_peer(ao, step, sign):
    z, y = ao // SIDE, ao % SIDE
    dz, dy = step // SIDE, step % SIDE
    return (z + SIDE + sign * dz) % SIDE * SIDE + (y + SIDE + sign * dy) % SIDE


def greet():
    fit, ao = lax.axis_index("fit"), lax.axis_index("ao")
    barrier = pltpu.get_barrier_semaphore()

    def to_fit(i, carry):
        pl.semaphore_signal(barrier, inc=1, device_id=((fit + i) % NF, ao), device_id_type=MESH)
        return carry

    def to_ao(i, carry):
        pl.semaphore_signal(barrier, inc=1, device_id=(fit, ao_peer(ao, i, 1)), device_id_type=MESH)
        return carry

    lax.fori_loop(1, NF, to_fit, 0)
    lax.fori_loop(1, NA, to_ao, 0)
    pl.semaphore_wait(barrier, NF - 1 + NA - 1)
    return fit, ao


def each(start, stop, body):
    def step(i, carry):
        body(i)
        return carry

    lax.fori_loop(start, stop, step, 0)


def coeff_kernel(owner_ref, occ_ref, out_ref, own, first, piece, second, whole, done, s1, r1, s2, r2, s3, r3):
    fit, ao = greet()
    me = fit * NA + ao
    rows = W // 4
    for which in range(2):
        keep = jnp.where(owner_ref[which] == me, 1.0, 0.0).astype(jnp.float32)
        block = (occ_ref[...].astype(jnp.float32) * keep).astype(jnp.bfloat16)
        own[pl.ds(which * 4, 4)] = block.reshape(4, rows, W)

    def hop1(i):
        peer = (fit + i) % NF
        return pltpu.make_async_remote_copy(
            src_ref=own.at[peer], dst_ref=first.at[i], send_sem=s1.at[i], recv_sem=r1.at[i],
            device_id=(peer, ao), device_id_type=MESH)

    def hop2(i):
        return pltpu.make_async_remote_copy(
            src_ref=piece, dst_ref=second.at[i], send_sem=s2.at[i], recv_sem=r2.at[i],
            device_id=(fit, ao_peer(ao, i, 1)), device_id_type=MESH)

    def hop3(i):
        return pltpu.make_async_remote_copy(
            src_ref=whole, dst_ref=done.at[i], send_sem=s3.at[i], recv_sem=r3.at[i],
            device_id=((fit + i) % NF, ao), device_id_type=MESH)

    each(1, NF, lambda i: hop1(i).start())
    each(1, NF, lambda i: hop1(i).wait_recv())
    total = own[fit].astype(jnp.float32)
    for i in range(1, NF):
        total = total + first[i].astype(jnp.float32)
    piece[...] = total.astype(jnp.bfloat16)
    each(1, NA, lambda i: hop2(i).start())
    each(1, NA, lambda i: hop2(i).wait_recv())
    for i in range(1, NA):
        total = total + second[i].astype(jnp.float32)
    whole[...] = total.astype(jnp.bfloat16)
    each(1, NF, lambda i: hop3(i).start())
    out_ref[fit] = whole[...]
    each(1, NF, lambda i: hop3(i).wait_recv())

    def put(i):
        out_ref[(fit + NF - i) % NF] = done[i]

    each(1, NF, put)
    each(1, NF, lambda i: hop1(i).wait_send())
    each(1, NA, lambda i: hop2(i).wait_send())
    each(1, NF, lambda i: hop3(i).wait_send())


def gather_coeff(occ_owner, occ):
    rows = W // 4
    piece = (rows, W)
    out = pl.pallas_call(
        coeff_kernel,
        out_shape=jax.ShapeDtypeStruct((NF, rows, W), jnp.bfloat16),
        in_specs=[pl.BlockSpec(memory_space=pltpu.SMEM), pl.BlockSpec(memory_space=pltpu.VMEM)],
        out_specs=pl.BlockSpec(memory_space=pltpu.VMEM),
        scratch_shapes=[
            pltpu.VMEM((NF,) + piece, jnp.bfloat16),
            pltpu.VMEM((NF,) + piece, jnp.bfloat16),
            pltpu.VMEM(piece, jnp.bfloat16),
            pltpu.VMEM((NA,) + piece, jnp.bfloat16),
            pltpu.VMEM(piece, jnp.bfloat16),
            pltpu.VMEM((NF,) + piece, jnp.bfloat16),
            pltpu.SemaphoreType.DMA((NF,)), pltpu.SemaphoreType.DMA((NF,)),
            pltpu.SemaphoreType.DMA((NA,)), pltpu.SemaphoreType.DMA((NA,)),
            pltpu.SemaphoreType.DMA((NF,)), pltpu.SemaphoreType.DMA((NF,)),
        ],
        compiler_params=pltpu.CompilerParams(collective_id=0, has_side_effects=True),
        name="coeff",
    )(occ_owner, occ)
    return out.reshape(2, W, W)


def fock_kernel(tab_ref, slot_ref, gram_ref, out_ref, send, recv, bsend, brecv, sa, ra, sb, rb):
    fit, ao = greet()

    def hop_a(c, i):
        return pltpu.make_async_remote_copy(
            src_ref=send.at[c, i], dst_ref=recv.at[c, i], send_sem=sa.at[c, i], recv_sem=ra.at[c, i],
            device_id=(fit, ao_peer(ao, i, 1)), device_id_type=MESH)

    def hop_b(c, i):
        peer = (fit + i) % NF
        return pltpu.make_async_remote_copy(
            src_ref=bsend.at[c, peer], dst_ref=brecv.at[c, i], send_sem=sb.at[c, i], recv_sem=rb.at[c, i],
            device_id=(peer, ao), device_id_type=MESH)

    def fill(c, i, where_to):
        owner = ao_peer(ao, i, 1)
        for r in range(CAP):
            tile = tab_ref[owner * CAP + r]
            where_to[c, i, pl.ds(r * ROWS, ROWS)] = gram_ref[tile, pl.ds(c * ROWS, ROWS)]
            slot = slot_ref[owner * CAP + r].astype(jnp.float32)
            where_to[c, i, pl.ds(CAP * ROWS + r * 8, 8)] = jnp.full((8, W), slot, jnp.float32)

    for c in range(CHUNKS):
        def push(i, c=c):
            fill(c, i, send)
            hop_a(c, i).start()

        each(1, NA, push)
        fill(c, 0, recv)

    places = lax.broadcasted_iota(jnp.int32, (SLOTS, 8, W), 0).astype(jnp.float32)
    for c in range(CHUNKS):
        each(1, NA, lambda i, c=c: hop_a(c, i).wait_recv())

        def band(b, c=c):
            def add(i, acc):
                for r in range(CAP):
                    tile = recv[c, i, pl.ds(r * ROWS + b * 8, 8)]
                    slot = recv[c, i, pl.ds(CAP * ROWS + r * 8, 8)]
                    acc = acc + jnp.where(slot[None] == places, tile[None], 0.0)
                return acc

            acc = lax.fori_loop(0, NA, add, jnp.zeros((SLOTS, 8, W), jnp.float32))
            bsend[c, :, :, pl.ds(b * 8, 8)] = acc.reshape(NF, 2, 8, W)

        each(0, ROWS // 8, band)
        each(1, NF, lambda i, c=c: hop_b(c, i).start())

    for c in range(CHUNKS):
        each(1, NF, lambda i, c=c: hop_b(c, i).wait_recv())
        total = bsend[c, fit]
        for i in range(1, NF):
            total = total + brecv[c, i]
        out_ref[:, pl.ds(c * ROWS, ROWS)] = total

    for c in range(CHUNKS):
        each(1, NA, lambda i, c=c: hop_a(c, i).wait_send())
        each(1, NF, lambda i, c=c: hop_b(c, i).wait_send())


def spread_fock(tab, slot, gram):
    return pl.pallas_call(
        fock_kernel,
        out_shape=jax.ShapeDtypeStruct((2, W, W), jnp.float32),
        in_specs=[pl.BlockSpec(memory_space=pltpu.SMEM), pl.BlockSpec(memory_space=pltpu.SMEM),
                  pl.BlockSpec(memory_space=pltpu.VMEM)],
        out_specs=pl.BlockSpec(memory_space=pltpu.VMEM),
        scratch_shapes=[
            pltpu.VMEM((CHUNKS, NA, CAP * (ROWS + 8), W), jnp.float32),
            pltpu.VMEM((CHUNKS, NA, CAP * (ROWS + 8), W), jnp.float32),
            pltpu.VMEM((CHUNKS, NF, 2, ROWS, W), jnp.float32),
            pltpu.VMEM((CHUNKS, NF, 2, ROWS, W), jnp.float32),
            pltpu.SemaphoreType.DMA((CHUNKS, NA)), pltpu.SemaphoreType.DMA((CHUNKS, NA)),
            pltpu.SemaphoreType.DMA((CHUNKS, NF)), pltpu.SemaphoreType.DMA((CHUNKS, NF)),
        ],
        compiler_params=pltpu.CompilerParams(
            collective_id=1, has_side_effects=True, vmem_limit_bytes=32 << 20),
        name="fock",
    )(tab, slot, gram)


def places_of(owners, slots):
    tiles = jnp.arange(16, dtype=jnp.int32)
    same = owners[:, None] == owners[None, :]
    rank = jnp.sum(jnp.where(same & (tiles[None, :] < tiles[:, None]), 1, 0), axis=1)
    place = owners * CAP + rank
    hit = place[None, :] == jnp.arange(NA * CAP, dtype=jnp.int32)[:, None]
    tab = jnp.sum(jnp.where(hit, tiles[None, :], 0), axis=1)
    slot = jnp.sum(jnp.where(hit, slots[None, :] + 1, 0), axis=1) - 1
    return tab.astype(jnp.int32), slot.astype(jnp.int32)


def on_device(three_index, occ_coeff, occ_owner, screen, tile_owner, tile_slot):
    pair = gather_coeff(occ_owner, occ_coeff[0])
    coeff = jnp.concatenate([pair[0], pair[1]], axis=1)
    mub = three_index.shape[0]
    width = three_index.shape[2]
    half = jnp.einsum("jvmp,vi->jmpi", three_index, coeff, preferred_element_type=jnp.float32)
    half = (half * screen[:, 0].astype(jnp.float32)[:, None, None, None]).astype(jnp.bfloat16)
    flat = half.reshape(mub, width, -1)
    gram = jnp.einsum("jmx,knx->jkmn", flat, flat, preferred_element_type=jnp.float32)
    gram = gram.reshape(mub * mub, width, width)
    tab, slot = places_of(tile_owner[:, 0], tile_slot)
    return spread_fock(tab, slot, gram)


def solution(mesh):
    in_specs = (
        P("ao", None, None, "fit"),
        P(("fit", "ao"), None, None),
        P(),
        P("ao", "fit"),
        P(("fit", "ao"), None),
        P(("fit", "ao")),
    )
    out_specs = P(("fit", "ao"), None, None)
    return jax.shard_map(
        on_device, mesh=mesh, in_specs=in_specs, out_specs=out_specs, check_vma=False
    )
```

time: 901 us -> 142 us (0.16)
  waiting for transfers between devices: 783 us -> 0 us
  Pallas kernels: 0 us -> 66.4 us
  local copies, waits for them, and re-layouts: 46.2 us -> 25.3 us
  between operations: 14.7 us -> 0.04 us
    reduce_scatter x1 -> x0, waiting for transfers between devices: 668 us -> none  [on_device(): lax.psum_scatter(dense, ('fit', 'ao'), scatter_dimension=0, tiled=True)]
    psum x1 -> x0, waiting for transfers between devices: 115 us -> none  [spread(): return lax.psum(kept, axis)]
    pallas_call x0 -> x2, Pallas kernels: none -> 66.4 us  [the longest x1 44.5 us: spread_fock(): pl.pallas_call(fock_kernel, out_shape=jax.ShapeDtypeStruct((2, W, W), jnp...]
    dot_general x1 -> x0, local copies, waits for them, and re-layouts: 20 us -> none  [on_device(): jnp.dot(table, gram, precision=lax.Precision.HIGHEST)]
  transfers between devices with their start and end apart: 2 -> 0, of which waited for: 2 -> 0; matrix products, arithmetic and copies ran while one was open for 3% -> 0% of each run, Pallas kernels for 0% -> 0%
where the time goes in v1:
time: 142 us; the launch traced here: 140 us
  Pallas kernels  66.4 us (47%)
  matrix products  45.8 us (32%)
  local copies, waits for them, and re-layouts  25.3 us (18%)
  other arithmetic  2.34 us (2%)
    pallas_call x1, Pallas kernels, spread_fock(): pl.pallas_call(fock_kernel, out_shape=jax.ShapeDtypeStruct((2, W, W), jnp...  44.5 us
    dot_general x1, matrix products, on_device(): jnp.einsum('jmx,knx->jkmn', flat, flat, preferred_element_type=jnp.float32)  26 us
    unnamed x2, local copies, waits for them, and re-layouts  24.2 us
    pallas_call x1, Pallas kernels, gather_coeff(): pl.pallas_call(coeff_kernel, out_shape=jax.ShapeDtypeStruct((NF, rows, W)...  21.9 us
    dot_general x1, matrix products, on_device(): jnp.einsum('jvmp,vi->jmpi', three_index, coeff, preferred_element_type=jn...  19.8 us

profile of v1, /device:TPU:0, one launch (start us, length us, event | category | flops | bytes accessed | tf_op | source)
XLA Modules:
  0.0 139.9 jit_solution(15319120792089233246)
XLA Ops:
  0.0 0.7 convert_bitcast_fusion
  0.7 0.9 select_reduce_fusion.2
  1.6 0.7 multiply_add_fusion
  2.2 0.1 select_reduce_fusion
  2.3 21.9 %coeff.1 = bf16[8,32,128]{2,1,0:T(8,128)(2,1)} custom-call(s32[2]{0:T(128)} %owner_ref.1, bf16[128,128]{1,0:T(8,128)(2,1)} %bitcast.35), custom_call_target="tpu_custom_call" | custom-call | tf_op jit(solution)/shard_map/coeff/pallas_call | solution.py:105
  24.2 0.8 fusion.12
  25.0 23.6 %copy.10 = bf16[4,128,128,128]{2,1,3,0:T(8,128)(2,1)} copy(bf16[4,128,128,128]{3,2,1,0:T(8,128)(2,1)} %param.6) | data formatting | bytes 33554432 | tf_op args[0]
  48.6 19.8 %multiply_convert_fusion = bf16[256,4,128,128]{0,2,3,1:T(8,128)(2,1)} fusion(bf16[4,128,128,128]{2,1,3,0:T(8,128)(2,1)} %copy.10, f32[4]{0:T(128)S(1)} %convert_bitcast_fusion, bf16[128,128]{1,0:T(8,128)(2,1)S(1)} %bitcast.34, bf16[128,128]{1,0:T(8,128)(2,1)S(1)} %bitcast.33), kind=kOutput, calls=%fused_computation | convolution fusion | flops 4328652800 | bytes 50397200 | tf_op jit(solution)/shard_map/jvmp,vi->jmpi/dot_general | solution.py:224
  68.4 26.0 %fusion.3 = f32[4,4,128,128]{2,3,0,1:T(8,128)S(1)} fusion(bf16[256,4,128,128]{0,2,3,1:T(8,128)(2,1)} %multiply_convert_fusion), kind=kOutput, calls=%fused_computation.4 | convolution fusion | flops 17179869184 | bytes 34603008 | tf_op jit(solution)/shard_map/jmx,knx->jkmn/dot_general | solution.py:227
  94.4 0.3 copy.8
  94.8 44.5 %fock.1 = f32[2,128,128]{2,1,0:T(8,128)S(1)} custom-call(s32[32]{0:T(128)S(1)} %get-tuple-element.6.tab_ref, s32[32]{0:T(128)S(1)} %broadcast_add_fusion.slot_ref, f32[16,128,128]{2,1,0:T(8,128)S(1)} %bitcast.32), custom_call_target="tpu_custom_call" | custom-call | tf_op jit(solution)/shard_map/fock/pallas_call | solution.py:188
  139.3 0.7 copy.14
  (1 shorter events, 0.0 us)

commit v2 on v0

v2 whole, which is shorter than its diff:
```python
import jax
import jax.numpy as jnp
from jax import lax
from jax.experimental import pallas as pl
from jax.experimental.pallas import tpu as pltpu
from jax.sharding import PartitionSpec as P

MESH = pl.DeviceIdType.MESH
F32, BF16 = jnp.float32, jnp.bfloat16
NF, NA, SIDE = 8, 16, 4
MUB, TILES, SLOTS, CAP = 4, 16, 16, 2
W = 128
ORB = 2 * W
PIECE = W // 4
CHUNKS = 2
ROWS = W // CHUNKS
BAND = 32
BANDS = W // BAND
DEEP = 32
NT = (((1,), (1,)), ((), ()))


def each(start, stop, body):
    def step(i, carry):
        body(i)
        return carry

    lax.fori_loop(start, stop, step, 0)


def whole_kernel(
    owner_ref, screen_ref, tile_owner_ref, tile_slot_ref, occ_ref, three_ref, out_ref,
    three, half, acc, gram, own, first, piece, second, both, done, coeff,
    slots_out, slots_in, send, recv, bsend, brecv, tab, qtab,
    load, s1, r1, s2, r2, s3, r3, sm, rm, sa, ra, sb, rb,
):
    fit, ao = lax.axis_index("fit"), lax.axis_index("ao")
    me = fit * NA + ao
    z, y = lax.div(ao, SIDE), lax.rem(ao, SIDE)

    def fit_peer(i):
        return lax.rem(fit + i, NF)

    def ao_peer(i):
        return lax.rem(z + lax.div(i, SIDE), SIDE) * SIDE + lax.rem(y + lax.rem(i, SIDE), SIDE)

    def fetch(u):
        j, b = lax.div(u, BANDS), lax.rem(u, BANDS)
        rows = pl.ds(pl.multiple_of(b * BAND, BAND), BAND)
        return pltpu.make_async_copy(three_ref.at[j, :, rows], three.at[j, :, rows], load.at[u])

    each(0, MUB * BANDS, lambda u: fetch(u).start())

    barrier = pltpu.get_barrier_semaphore()

    def greet_fit(i):
        pl.semaphore_signal(barrier, inc=1, device_id=(fit_peer(i), ao), device_id_type=MESH)

    def greet_ao(i):
        pl.semaphore_signal(barrier, inc=1, device_id=(fit, ao_peer(i)), device_id_type=MESH)

    each(1, NF, greet_fit)
    each(1, NA, greet_ao)

    flipped = occ_ref[...].astype(F32).T
    for which in range(2):
        keep = jnp.where(owner_ref[which] == me, 1.0, 0.0).astype(F32)
        own[pl.ds(which * 4, 4)] = (flipped * keep).astype(BF16).reshape(4, PIECE, W)

    pl.semaphore_wait(barrier, NF - 1 + NA - 1)

    def hop1(i):
        peer = fit_peer(i)
        return pltpu.make_async_remote_copy(
            src_ref=own.at[peer], dst_ref=first.at[i], send_sem=s1.at[i], recv_sem=r1.at[i],
            device_id=(peer, ao), device_id_type=MESH)

    def hop2(i):
        return pltpu.make_async_remote_copy(
            src_ref=piece, dst_ref=second.at[i], send_sem=s2.at[i], recv_sem=r2.at[i],
            device_id=(fit, ao_peer(i)), device_id_type=MESH)

    def hop3(i):
        return pltpu.make_async_remote_copy(
            src_ref=both, dst_ref=done.at[i], send_sem=s3.at[i], recv_sem=r3.at[i],
            device_id=(fit_peer(i), ao), device_id_type=MESH)

    def hop_m(i):
        return pltpu.make_async_remote_copy(
            src_ref=slots_out.at[i], dst_ref=slots_in.at[i], send_sem=sm.at[i], recv_sem=rm.at[i],
            device_id=(fit, ao_peer(i)), device_id_type=MESH)

    def hop_a(c, i):
        return pltpu.make_async_remote_copy(
            src_ref=send.at[c, i], dst_ref=recv.at[c, i], send_sem=sa.at[c, i], recv_sem=ra.at[c, i],
            device_id=(fit, ao_peer(i)), device_id_type=MESH)

    def hop_b(c, i):
        peer = fit_peer(i)
        return pltpu.make_async_remote_copy(
            src_ref=bsend.at[c, peer], dst_ref=brecv.at[c, i], send_sem=sb.at[c, i], recv_sem=rb.at[c, i],
            device_id=(peer, ao), device_id_type=MESH)

    each(1, NF, lambda i: hop1(i).start())

    def look(owner):
        count = jnp.int32(0)
        tile = [jnp.int32(0), jnp.int32(0)]
        slot = [jnp.int32(-1), jnp.int32(-1)]
        for t in range(TILES):
            hit = tile_owner_ref[t] == owner
            for r in range(CAP):
                here = jnp.logical_and(hit, count == r)
                tile[r] = jnp.where(here, t, tile[r])
                slot[r] = jnp.where(here, tile_slot_ref[t], slot[r])
            count = count + jnp.where(hit, 1, 0)
        for r in range(CAP):
            tab[owner * CAP + r] = tile[r]
            qtab[owner * CAP + r] = slot[r]

    each(0, NA, look)

    each(1, NF, lambda i: hop1(i).wait_recv())
    total = own[fit].astype(F32)
    for i in range(1, NF):
        total = total + first[i].astype(F32)
    piece[...] = total.astype(BF16)
    each(1, NA, lambda i: hop2(i).start())

    def tell(i, where_to):
        owner = ao_peer(i)
        for r in range(CAP):
            slot = qtab[owner * CAP + r].astype(F32)
            where_to[i, pl.ds(r * 8, 8)] = jnp.full((8, W), slot, F32)

    each(1, NA, lambda i: tell(i, slots_out))
    tell(jnp.int32(0), slots_in)

    each(1, NA, lambda i: hop2(i).wait_recv())
    for i in range(1, NA):
        total = total + second[i].astype(F32)
    both[...] = total.astype(BF16)
    each(1, NF, lambda i: hop3(i).start())
    each(1, NA, lambda i: hop_m(i).start())
    coeff[fit] = both[...]
    each(1, NF, lambda i: hop3(i).wait_recv())

    def put(i):
        coeff[lax.rem(fit + NF - i, NF)] = done[i]

    each(1, NF, put)

    def product(u):
        fetch(u).wait()
        j, b = lax.div(u, BANDS), lax.rem(u, BANDS)
        rows = pl.ds(pl.multiple_of(b * BAND, BAND), BAND)
        block = jnp.swapaxes(three[j, :, rows, :], 0, 1)
        orbitals = coeff[...].reshape(ORB, W)
        parts = []
        for m in range(0, BAND, 2):
            pair = jnp.concatenate([block[m], block[m + 1]], 1)
            r = jnp.dot(orbitals, pair, preferred_element_type=F32).astype(BF16)
            parts += [r[:, :W], r[:, W:]]
        half[j, :, rows, :] = jnp.swapaxes(jnp.stack(parts, 0), 0, 1)

    each(0, MUB * BANDS, product)

    def rows_of(first_orbital, lo, n):
        return jnp.concatenate(
            [half[:, first_orbital + v, lo:lo + n, :].reshape(MUB * n, W) for v in range(DEEP)], 1)

    def fill(c, i, where_to):
        owner = ao_peer(i)
        for r in range(CAP):
            where_to[c, i, pl.ds(r * ROWS, ROWS)] = gram[c, tab[owner * CAP + r]]

    for c in range(CHUNKS):
        acc[...] = jnp.zeros_like(acc)

        def deep(i, c=c):
            acc[...] += lax.dot_general(
                rows_of(i * DEEP, c * ROWS, ROWS), rows_of(i * DEEP, 0, W), NT,
                preferred_element_type=F32)

        each(0, ORB // DEEP, deep)
        for j in range(MUB):
            for k in range(MUB):
                keep = (screen_ref[j] * screen_ref[k]).astype(F32)
                gram[c, j * MUB + k] = acc[j * ROWS:(j + 1) * ROWS, k * W:(k + 1) * W] * keep

        def push(i, c=c):
            fill(c, i, send)
            hop_a(c, i).start()

        each(1, NA, push)
        fill(c, jnp.int32(0), recv)

    each(1, NA, lambda i: hop_m(i).wait_recv())
    places = lax.broadcasted_iota(jnp.int32, (SLOTS, 8, W), 0).astype(F32)
    for c in range(CHUNKS):
        each(1, NA, lambda i, c=c: hop_a(c, i).wait_recv())

        def band(b, c=c):
            def add(i, sums):
                for r in range(CAP):
                    tile = recv[c, i, pl.ds(r * ROWS + b * 8, 8)]
                    slot = slots_in[i, pl.ds(r * 8, 8)]
                    sums = sums + jnp.where(slot[None] == places, tile[None], 0.0)
                return sums

            sums = lax.fori_loop(0, NA, add, jnp.zeros((SLOTS, 8, W), F32))
            bsend[c, :, :, pl.ds(b * 8, 8)] = sums.reshape(NF, 2, 8, W)

        each(0, ROWS // 8, band)
        each(1, NF, lambda i, c=c: hop_b(c, i).start())

    for c in range(CHUNKS):
        each(1, NF, lambda i, c=c: hop_b(c, i).wait_recv())
        sums = bsend[c, fit]
        for i in range(1, NF):
            sums = sums + brecv[c, i]
        out_ref[:, pl.ds(c * ROWS, ROWS)] = sums

    each(1, NF, lambda i: hop1(i).wait_send())
    each(1, NA, lambda i: hop2(i).wait_send())
    each(1, NF, lambda i: hop3(i).wait_send())
    each(1, NA, lambda i: hop_m(i).wait_send())
    for c in range(CHUNKS):
        each(1, NA, lambda i, c=c: hop_a(c, i).wait_send())
        each(1, NF, lambda i, c=c: hop_b(c, i).wait_send())


def on_device(three_index, occ_coeff, occ_owner, screen, tile_owner, tile_slot):
    smem = pl.BlockSpec(memory_space=pltpu.SMEM)
    vmem = pl.BlockSpec(memory_space=pltpu.VMEM)
    dma = pltpu.SemaphoreType.DMA
    part = (PIECE, W)
    return pl.pallas_call(
        whole_kernel,
        out_shape=jax.ShapeDtypeStruct((2, W, W), F32),
        in_specs=[smem, smem, smem, smem, vmem, pl.BlockSpec(memory_space=pl.ANY)],
        out_specs=vmem,
        scratch_shapes=[
            pltpu.VMEM((MUB, W, W, W), BF16),
            pltpu.VMEM((MUB, ORB, W, W), BF16),
            pltpu.VMEM((MUB * ROWS, MUB * W), F32),
            pltpu.VMEM((CHUNKS, TILES, ROWS, W), F32),
            pltpu.VMEM((NF,) + part, BF16),
            pltpu.VMEM((NF,) + part, BF16),
            pltpu.VMEM(part, BF16),
            pltpu.VMEM((NA,) + part, BF16),
            pltpu.VMEM(part, BF16),
            pltpu.VMEM((NF,) + part, BF16),
            pltpu.VMEM((NF,) + part, BF16),
            pltpu.VMEM((NA, CAP * 8, W), F32),
            pltpu.VMEM((NA, CAP * 8, W), F32),
            pltpu.VMEM((CHUNKS, NA, CAP * ROWS, W), F32),
            pltpu.VMEM((CHUNKS, NA, CAP * ROWS, W), F32),
            pltpu.VMEM((CHUNKS, NF, 2, ROWS, W), F32),
            pltpu.VMEM((CHUNKS, NF, 2, ROWS, W), F32),
            pltpu.SMEM((NA * CAP,), jnp.int32),
            pltpu.SMEM((NA * CAP,), jnp.int32),
            dma((MUB * BANDS,)),
            dma((NF,)), dma((NF,)), dma((NA,)), dma((NA,)), dma((NF,)), dma((NF,)),
            dma((NA,)), dma((NA,)),
            dma((CHUNKS, NA)), dma((CHUNKS, NA)), dma((CHUNKS, NF)), dma((CHUNKS, NF)),
        ],
        compiler_params=pltpu.CompilerParams(
            collective_id=0, has_side_effects=True, vmem_limit_bytes=60 << 20),
        name="exchange",
    )(occ_owner, screen[:, 0], tile_owner[:, 0], tile_slot, occ_coeff[0], three_index)


def solution(mesh):
    in_specs = (
        P("ao", None, None, "fit"),
        P(("fit", "ao"), None, None),
        P(),
        P("ao", "fit"),
        P(("fit", "ao"), None),
        P(("fit", "ao")),
    )
    out_specs = P(("fit", "ao"), None, None)
    return jax.shard_map(
        on_device, mesh=mesh, in_specs=in_specs, out_specs=out_specs, check_vma=False
    )
```

time: 901 us -> 97.1 us (0.11)
  waiting for transfers between devices: 783 us -> 0 us
  Pallas kernels: 0 us -> 93.9 us
  matrix products: 53.8 us -> 0 us
  local copies, waits for them, and re-layouts: 46.2 us -> 1.57 us
  between operations: 14.7 us -> 0.01 us
    reduce_scatter x1 -> x0, waiting for transfers between devices: 668 us -> none  [on_device(): lax.psum_scatter(dense, ('fit', 'ao'), scatter_dimension=0, tiled=True)]
    psum x1 -> x0, waiting for transfers between devices: 115 us -> none  [spread(): return lax.psum(kept, axis)]
    pallas_call x0 -> x1, Pallas kernels: none -> 93.9 us  [on_device(): pl.pallas_call(whole_kernel, out_shape=jax.ShapeDtypeStruct((2, W, W), F3...]
    dot_general x3 -> x0, matrix products: 53.8 us -> none  [the longest x1 27.5 us: on_device(): jnp.einsum('jmx,knx->jkmn', flat, flat, preferred_element_type=jnp.float32)]
    unnamed x2 -> x1, local copies, waits for them, and re-layouts: 24.5 us -> 1.57 us
    dot_general x1 -> x0, local copies, waits for them, and re-layouts: 20 us -> none  [on_device(): jnp.dot(table, gram, precision=lax.Precision.HIGHEST)]
  transfers between devices with their start and end apart: 2 -> 0, of which waited for: 2 -> 0; matrix products, arithmetic and copies ran while one was open for 3% -> 0% of each run, Pallas kernels for 0% -> 0%
where the time goes in v2:
time: 97.1 us; the launch traced here: 95.5 us
  Pallas kernels  93.9 us (97%)
  local copies, waits for them, and re-layouts  1.57 us (2%)
    pallas_call x1, Pallas kernels, on_device(): pl.pallas_call(whole_kernel, out_shape=jax.ShapeDtypeStruct((2, W, W), F3...  93.9 us

profile of v2, /device:TPU:0, one launch (start us, length us, event | category | flops | bytes accessed | tf_op | source)
XLA Modules:
  0.0 95.5 jit_solution(650474363333969980)
XLA Ops:
  0.0 93.9 %exchange.1 = f32[2,128,128]{2,1,0:T(8,128)} custom-call(s32[2]{0:T(128)} %owner_ref.1, s32[4]{0:T(128)} %bitcast.4, s32[16]{0:T(128)} %bitcast.5, s32[16]{0:T(128)} %tile_slot_ref.1, bf16[128,128]{1,0:T(8,128)(2,1)} %bitcast.3, bf16[4,128,128,128]{3,2,1,0:T(8,128)(2,1)} %three_ref.1), custom_call_target="tpu_custom_call" | custom-call | tf_op jit(solution)/shard_map/exchange/pallas_call | solution.py:238
  93.9 1.6 %copy.8 = f32[2,128,128]{2,1,0:T(8,128)} copy(f32[2,128,128]{2,1,0:T(8,128)} %exchange.1) | data formatting | bytes 262144

commit v3 on v2

v3 whole, which is shorter than its diff:
```python
import jax
import jax.numpy as jnp
from jax import lax
from jax.experimental import pallas as pl
from jax.experimental.pallas import tpu as pltpu
from jax.sharding import PartitionSpec as P

MESH = pl.DeviceIdType.MESH
F32, BF16 = jnp.float32, jnp.bfloat16
NF, NA, SIDE = 8, 16, 4
MUB, TILES, SLOTS, CAP = 4, 16, 16, 2
W = 128
ORB = 2 * W
PIECE = W // 4
CHUNKS = 2
ROWS = W // CHUNKS
BAND = 16
BANDS = W // BAND
UNITS = MUB * BANDS
WIDE = 64
DEEP = 32
I16 = jnp.int16
HEAD = 16
CODED = ROWS + HEAD
TOP = 32766.0
STEP = 16.0
NT = (((1,), (1,)), ((), ()))


def each(start, stop, body):
    def step(i, carry):
        body(i)
        return carry

    lax.fori_loop(start, stop, step, 0)


def whole_kernel(
    owner_ref, screen_ref, tile_owner_ref, tile_slot_ref, occ_ref, three_ref, out_ref,
    half, flat, acc, late, gram, own, first, piece, second, both, done, coeff,
    scales, slots, send, recv, sums_of, bsend, brecv, tab,
    load, s1, r1, s2, r2, s3, r3, sa, ra, sb, rb,
):
    fit, ao = lax.axis_index("fit"), lax.axis_index("ao")
    me = fit * NA + ao
    z, y = lax.div(ao, SIDE), lax.rem(ao, SIDE)

    def fit_peer(i):
        return lax.rem(fit + i, NF)

    def ao_peer(i):
        return lax.rem(z + lax.div(i, SIDE), SIDE) * SIDE + lax.rem(y + lax.rem(i, SIDE), SIDE)

    def fetch(u):
        j, b = lax.div(u, BANDS), lax.rem(u, BANDS)
        rows = pl.ds(pl.multiple_of(b * BAND, BAND), BAND)
        return pltpu.make_async_copy(three_ref.at[j, :, rows], half.at[1, j, :, rows], load.at[u])

    each(0, UNITS, lambda u: fetch(u).start())

    barrier = pltpu.get_barrier_semaphore()

    def greet_fit(i):
        pl.semaphore_signal(barrier, inc=1, device_id=(fit_peer(i), ao), device_id_type=MESH)

    def greet_ao(i):
        pl.semaphore_signal(barrier, inc=1, device_id=(fit, ao_peer(i)), device_id_type=MESH)

    each(1, NF, greet_fit)
    each(1, NA, greet_ao)

    occ = occ_ref[...].astype(F32)
    for which in range(2):
        keep = jnp.where(owner_ref[which] == me, 1.0, 0.0).astype(F32)
        own[pl.ds(which * 4, 4)] = (occ * keep).astype(BF16).reshape(4, PIECE, W)

    def look(owner):
        count = jnp.int32(0)
        tile = [jnp.int32(TILES), jnp.int32(TILES)]
        for t in range(TILES):
            hit = tile_owner_ref[t] == owner
            for r in range(CAP):
                tile[r] = jnp.where(jnp.logical_and(hit, count == r), t, tile[r])
            count = count + jnp.where(hit, 1, 0)
        for r in range(CAP):
            tab[owner * CAP + r] = tile[r]

    def turn(u):
        fetch(u).wait()
        j, b = lax.div(u, BANDS), lax.rem(u, BANDS)
        rows = pl.ds(pl.multiple_of(b * BAND, BAND), BAND)
        block = jnp.swapaxes(half[1, j, :, rows, :], 0, 1)
        block = jnp.stack([block[m].T for m in range(BAND)], 0)
        flat[j, :, rows, :] = jnp.swapaxes(block, 0, 1)

    def turn_and_look(u):
        turn(u)
        look(u - 12)

    each(0, 6, turn)
    pl.semaphore_wait(barrier, NF - 1 + NA - 1)

    def hop1(i):
        peer = fit_peer(i)
        return pltpu.make_async_remote_copy(
            src_ref=own.at[peer], dst_ref=first.at[i], send_sem=s1.at[i], recv_sem=r1.at[i],
            device_id=(peer, ao), device_id_type=MESH)

    def hop2(i):
        return pltpu.make_async_remote_copy(
            src_ref=piece, dst_ref=second.at[i], send_sem=s2.at[i], recv_sem=r2.at[i],
            device_id=(fit, ao_peer(i)), device_id_type=MESH)

    def hop3(i):
        return pltpu.make_async_remote_copy(
            src_ref=both, dst_ref=done.at[i], send_sem=s3.at[i], recv_sem=r3.at[i],
            device_id=(fit_peer(i), ao), device_id_type=MESH)

    def hop_a(c, i):
        return pltpu.make_async_remote_copy(
            src_ref=send.at[c, i], dst_ref=recv.at[c, i], send_sem=sa.at[c, i], recv_sem=ra.at[c, i],
            device_id=(fit, ao_peer(i)), device_id_type=MESH)

    def hop_b(c, i):
        peer = fit_peer(i)
        return pltpu.make_async_remote_copy(
            src_ref=bsend.at[c, peer], dst_ref=brecv.at[c, i], send_sem=sb.at[c, i], recv_sem=rb.at[c, i],
            device_id=(peer, ao), device_id_type=MESH)

    each(1, NF, lambda i: hop1(i).start())
    each(6, 12, turn)

    each(1, NF, lambda i: hop1(i).wait_recv())
    total = own[fit].astype(F32)
    for i in range(1, NF):
        total = total + first[i].astype(F32)
    piece[...] = total.astype(BF16)
    each(1, NA, lambda i: hop2(i).start())

    each(0, NA, look)
    each(12, 22, turn)
    each(1, NA, lambda i: hop2(i).wait_recv())
    for i in range(1, NA):
        total = total + second[i].astype(F32)
    both[...] = total.astype(BF16)
    each(1, NF, lambda i: hop3(i).start())
    coeff[fit] = both[...]
    each(22, 32, turn)
    each(1, NF, lambda i: hop3(i).wait_recv())

    def put(i):
        coeff[lax.rem(fit + NF - i, NF)] = done[i]

    each(1, NF, put)

    pair = coeff[...].reshape(2, W, W)
    orbitals = jnp.concatenate([pair[0], pair[1]], 1)

    def product(v):
        j = lax.div(v, W // WIDE)
        some = pl.ds(pl.multiple_of(lax.rem(v, W // WIDE) * WIDE, WIDE), WIDE)
        r = jnp.dot(flat[j, some].reshape(WIDE * W, W), orbitals, preferred_element_type=F32)
        r = r.astype(BF16)
        half[0, j, some] = r[:, :W].reshape(WIDE, W, W)
        half[1, j, some] = r[:, W:].reshape(WIDE, W, W)

    each(0, MUB * W // WIDE, product)

    def rows_of(first, lo, n):
        return jnp.concatenate(
            [half[h, :, first + v, lo:lo + n, :].reshape(MUB * n, W)
             for h in range(2) for v in range(DEEP)], 1)

    head_row = lax.broadcasted_iota(jnp.int32, (HEAD, W), 0)

    def encode(tile, slot):
        top = jnp.maximum(jnp.max(jnp.abs(tile), axis=0, keepdims=True), 1e-33)
        level = jnp.ceil(jnp.log2(top) * STEP)
        values = jnp.round(tile * (TOP * jnp.exp2(level * (-1.0 / STEP))))
        head = jnp.where(head_row == 0, level.astype(jnp.int32), slot)
        return values.astype(jnp.int32).astype(I16), head.astype(I16)

    def decode_head(head):
        head = head.astype(jnp.int32).astype(F32)
        return jnp.exp2(head[0:1] * (1.0 / STEP)) * (1.0 / TOP), head[1:2]

    def decode(values):
        return values.astype(jnp.int32).astype(F32)

    def fill(c, i, where_to):
        owner = ao_peer(i)
        for r in range(CAP):
            where_to[c, i, pl.ds(r * CODED, CODED)] = gram[c, tab[owner * CAP + r]]

    def early_tile(j, k):
        return acc[j * ROWS:(j + 1) * ROWS, k * W:(k + 1) * W]

    def late_tile(j, k):
        other = late[k * ROWS:(k + 1) * ROWS, j // 2 * W:(j // 2 + 1) * W]
        if j % 2 == 0:
            other = pltpu.roll(other, ROWS, 1)
        column = jnp.concatenate([acc[k * ROWS:(k + 1) * ROWS, j * W:(j + 1) * W], other], 0)
        return column.T[ROWS:]

    for c in range(CHUNKS):
        if c == 0:
            acc[...] = jnp.zeros_like(acc)

            def deep(i):
                acc[...] += lax.dot_general(
                    rows_of(i * DEEP, 0, ROWS), rows_of(i * DEEP, 0, W), NT,
                    preferred_element_type=F32)
        else:
            late[...] = jnp.zeros_like(late)

            def deep(i):
                side = rows_of(i * DEEP, ROWS, ROWS)
                late[...] += lax.dot_general(side, side, NT, preferred_element_type=F32)

        each(0, W // DEEP, deep)
        tile_at = late_tile if c else early_tile
        for j in range(MUB):
            for k in range(MUB):
                keep = (screen_ref[j] * screen_ref[k]).astype(F32)
                t = j * MUB + k
                values, head = encode(tile_at(j, k) * keep, tile_slot_ref[t])
                gram[c, t, pl.ds(0, ROWS)] = values
                gram[c, t, pl.ds(ROWS, HEAD)] = head
        gram[c, TILES] = jnp.full((CODED, W), -1, jnp.int32).astype(I16)

        def push(i, c=c):
            fill(c, i, send)
            hop_a(c, i).start()

        each(1, NA, push)
        fill(c, jnp.int32(0), recv)

    for c in range(CHUNKS):
        each(1, NA, lambda i, c=c: hop_a(c, i).wait_recv())

        def heads(i, c=c):
            for r in range(CAP):
                scale, slot = decode_head(recv[c, i, pl.ds(r * CODED + ROWS, HEAD)])
                scales[i, pl.ds(r * 8, 8)] = jnp.broadcast_to(scale, (8, W))
                slots[i, pl.ds(r * 8, 8)] = jnp.broadcast_to(slot, (8, W))

        each(0, NA, heads)

        def band(b, c=c):
            for group in range(0, SLOTS, 8):
                def add(i, sums, group=group):
                    for r in range(CAP):
                        tile = decode(recv[c, i, pl.ds(r * CODED + b * 16, 16)]).reshape(2, 8, W)
                        tile = tile * scales[i, pl.ds(r * 8, 8)][None]
                        slot = slots[i, pl.ds(r * 8, 8)]
                        sums = [
                            sums[q] + jnp.where((slot == float(group + q))[None], tile, 0.0)
                            for q in range(8)]
                    return sums

                zero = jnp.zeros((2, 8, W), F32)
                sums = lax.fori_loop(0, NA, add, [zero] * 8, unroll=4)
                for q in range(8):
                    sums_of[c, group + q, pl.ds(b * 16, 16)] = sums[q].reshape(16, W)

        each(0, ROWS // 16, band)

        def pack(q, c=c):
            values, head = encode(sums_of[c, q], jnp.int32(0))
            place = lax.rem(q, 2) * CODED
            bsend[c, lax.div(q, 2), pl.ds(pl.multiple_of(place, 16), ROWS)] = values
            bsend[c, lax.div(q, 2), pl.ds(pl.multiple_of(place + ROWS, 16), HEAD)] = head

        each(0, SLOTS, pack)
        each(1, NF, lambda i, c=c: hop_b(c, i).start())

    for c in range(CHUNKS):
        each(1, NF, lambda i, c=c: hop_b(c, i).wait_recv())
        for q in range(2):
            sums = sums_of[c, fit * 2 + q]
            for i in range(1, NF):
                scale, _ = decode_head(brecv[c, i, pl.ds(q * CODED + ROWS, HEAD)])
                sums = sums + decode(brecv[c, i, pl.ds(q * CODED, ROWS)]) * scale
            out_ref[q, pl.ds(c * ROWS, ROWS)] = sums

    each(1, NF, lambda i: hop1(i).wait_send())
    each(1, NA, lambda i: hop2(i).wait_send())
    each(1, NF, lambda i: hop3(i).wait_send())
    for c in range(CHUNKS):
        each(1, NA, lambda i, c=c: hop_a(c, i).wait_send())
        each(1, NF, lambda i, c=c: hop_b(c, i).wait_send())


def on_device(three_index, occ_coeff, occ_owner, screen, tile_owner, tile_slot):
    smem = pl.BlockSpec(memory_space=pltpu.SMEM)
    vmem = pl.BlockSpec(memory_space=pltpu.VMEM)
    dma = pltpu.SemaphoreType.DMA
    part = (PIECE, W)
    return pl.pallas_call(
        whole_kernel,
        out_shape=jax.ShapeDtypeStruct((2, W, W), F32),
        in_specs=[smem, smem, smem, smem, vmem, pl.BlockSpec(memory_space=pl.ANY)],
        out_specs=vmem,
        scratch_shapes=[
            pltpu.VMEM((2, MUB, W, W, W), BF16),
            pltpu.VMEM((MUB, W, W, W), BF16),
            pltpu.VMEM((MUB * ROWS, MUB * W), F32),
            pltpu.VMEM((MUB * ROWS, MUB * ROWS), F32),
            pltpu.VMEM((CHUNKS, TILES + 1, CODED, W), I16),
            pltpu.VMEM((NF,) + part, BF16),
            pltpu.VMEM((NF,) + part, BF16),
            pltpu.VMEM(part, BF16),
            pltpu.VMEM((NA,) + part, BF16),
            pltpu.VMEM(part, BF16),
            pltpu.VMEM((NF,) + part, BF16),
            pltpu.VMEM((NF,) + part, BF16),
            pltpu.VMEM((NA, CAP * 8, W), F32),
            pltpu.VMEM((NA, CAP * 8, W), F32),
            pltpu.VMEM((CHUNKS, NA, CAP * CODED, W), I16),
            pltpu.VMEM((CHUNKS, NA, CAP * CODED, W), I16),
            pltpu.VMEM((CHUNKS, SLOTS, ROWS, W), F32),
            pltpu.VMEM((CHUNKS, NF, 2 * CODED, W), I16),
            pltpu.VMEM((CHUNKS, NF, 2 * CODED, W), I16),
            pltpu.SMEM((NA * CAP,), jnp.int32),
            dma((UNITS,)),
            dma((NF,)), dma((NF,)), dma((NA,)), dma((NA,)), dma((NF,)), dma((NF,)),
            dma((CHUNKS, NA)), dma((CHUNKS, NA)), dma((CHUNKS, NF)), dma((CHUNKS, NF)),
        ],
        compiler_params=pltpu.CompilerParams(
            collective_id=0, has_side_effects=True, vmem_limit_bytes=63 << 20),
        name="exchange",
    )(occ_owner, screen[:, 0], tile_owner[:, 0], tile_slot, occ_coeff[0], three_index)


def solution(mesh):
    in_specs = (
        P("ao", None, None, "fit"),
        P(("fit", "ao"), None, None),
        P(),
        P("ao", "fit"),
        P(("fit", "ao"), None),
        P(("fit", "ao")),
    )
    out_specs = P(("fit", "ao"), None, None)
    return jax.shard_map(
        on_device, mesh=mesh, in_specs=in_specs, out_specs=out_specs, check_vma=False
    )
```

time: 97.1 us -> 73 us (0.75)
  Pallas kernels: 93.9 us -> 70.1 us
    pallas_call x1, Pallas kernels: 93.9 us -> 70.1 us  [on_device(): pl.pallas_call(whole_kernel, out_shape=jax.ShapeDtypeStruct((2, W, W), F3...]
where the time goes in v3:
time: 73 us; the launch traced here: 71.6 us
  Pallas kernels  70.1 us (96%)
  local copies, waits for them, and re-layouts  1.57 us (2%)
    pallas_call x1, Pallas kernels, on_device(): pl.pallas_call(whole_kernel, out_shape=jax.ShapeDtypeStruct((2, W, W), F3...  70.1 us
    unnamed x1, local copies, waits for them, and re-layouts  1.57 us

profile of v3, /device:TPU:0, one launch (start us, length us, event | category | flops | bytes accessed | tf_op | source)
XLA Modules:
  0.0 71.6 jit_solution(2688012538068390101)
XLA Ops:
  0.0 70.1 %exchange.1 = f32[2,128,128]{2,1,0:T(8,128)} custom-call(s32[2]{0:T(128)} %owner_ref.1, s32[4]{0:T(128)} %bitcast.4, s32[16]{0:T(128)} %bitcast.5, s32[16]{0:T(128)} %tile_slot_ref.1, bf16[128,128]{1,0:T(8,128)(2,1)} %bitcast.3, bf16[4,128,128,128]{3,2,1,0:T(8,128)(2,1)} %three_ref.1), custom_call_target="tpu_custom_call" | custom-call | tf_op jit(solution)/shard_map/exchange/pallas_call | solution.py:299
  70.1 1.6 %copy.8 = f32[2,128,128]{2,1,0:T(8,128)} copy(f32[2,128,128]{2,1,0:T(8,128)} %exchange.1) | data formatting | bytes 262144

commit v4 on v3

v4 whole, which is shorter than its diff:
```python
import jax
import jax.numpy as jnp
from jax import lax
from jax.experimental import pallas as pl
from jax.experimental.pallas import tpu as pltpu
from jax.sharding import PartitionSpec as P

MESH = pl.DeviceIdType.MESH
F32, BF16 = jnp.float32, jnp.bfloat16
NF, NA, SIDE = 8, 16, 4
MUB, TILES, SLOTS, CAP = 4, 16, 16, 2
W = 128
ORB = 2 * W
PIECE = W // 4
PARTS = 4
ROWS = W // 2
BAND = 16
BANDS = W // BAND
UNITS = MUB * BANDS
WIDE = 128
DEEP = 32
I16 = jnp.int16
HEAD = 16
CODED = ROWS + HEAD
TOP = 32766.0
STEP = 16.0
NT = (((1,), (1,)), ((), ()))


def every(start, stop, body):
    for i in range(start, stop):
        body(i)


def each(start, stop, body):
    def step(i, carry):
        body(i)
        return carry

    lax.fori_loop(start, stop, step, 0)


def whole_kernel(
    owner_ref, screen_ref, tile_owner_ref, tile_slot_ref, occ_ref, three_ref, out_ref,
    half, flat, acc, gram, own, first, piece, second, both, done, coeff,
    scales, slots, send, recv, sums_of, mine, bsend, brecv, tab,
    load, s1, r1, s2, r2, s3, r3, sa, ra, sb, rb,
):
    fit, ao = lax.axis_index("fit"), lax.axis_index("ao")
    me = fit * NA + ao
    z, y = lax.div(ao, SIDE), lax.rem(ao, SIDE)

    def fit_peer(i):
        return lax.rem(fit + i, NF)

    def ao_peer(i):
        dz, dy = (i // SIDE, i % SIDE) if isinstance(i, int) else (lax.div(i, SIDE), lax.rem(i, SIDE))
        return lax.rem(z + dz, SIDE) * SIDE + lax.rem(y + dy, SIDE)

    def fetch(u):
        j, b = lax.div(u, BANDS), lax.rem(u, BANDS)
        rows = pl.ds(pl.multiple_of(b * BAND, BAND), BAND)
        return pltpu.make_async_copy(three_ref.at[j, :, rows], half.at[1, j, :, rows], load.at[u])

    each(0, UNITS, lambda u: fetch(u).start())

    barrier = pltpu.get_barrier_semaphore()

    def greet_fit(i):
        pl.semaphore_signal(barrier, inc=1, device_id=(fit_peer(i), ao), device_id_type=MESH)

    def greet_ao(i):
        pl.semaphore_signal(barrier, inc=1, device_id=(fit, ao_peer(i)), device_id_type=MESH)

    every(1, NF, greet_fit)
    every(1, NA, greet_ao)

    occ = occ_ref[...].astype(F32)
    for which in range(2):
        keep = jnp.where(owner_ref[which] == me, 1.0, 0.0).astype(F32)
        own[pl.ds(which * 4, 4)] = (occ * keep).astype(BF16).reshape(4, PIECE, W)

    def look(owner):
        count = jnp.int32(0)
        tile = [jnp.int32(TILES), jnp.int32(TILES)]
        for t in range(TILES):
            hit = tile_owner_ref[t] == owner
            for r in range(CAP):
                tile[r] = jnp.where(jnp.logical_and(hit, count == r), t, tile[r])
            count = count + jnp.where(hit, 1, 0)
        for r in range(CAP):
            tab[owner * CAP + r] = tile[r]

    def turn(u):
        fetch(u).wait()
        j, b = lax.div(u, BANDS), lax.rem(u, BANDS)
        rows = pl.ds(pl.multiple_of(b * BAND, BAND), BAND)
        block = jnp.swapaxes(half[1, j, :, rows, :], 0, 1)
        block = jnp.stack([block[m].T for m in range(BAND)], 0)
        flat[j, :, rows, :] = jnp.swapaxes(block, 0, 1)

    def turn_and_look(u):
        turn(u)
        look(u - 12)

    each(0, 6, turn)
    pl.semaphore_wait(barrier, NF - 1 + NA - 1)

    def hop1(i):
        peer = fit_peer(i)
        return pltpu.make_async_remote_copy(
            src_ref=own.at[peer], dst_ref=first.at[i], send_sem=s1.at[i], recv_sem=r1.at[i],
            device_id=(peer, ao), device_id_type=MESH)

    def hop2(i):
        return pltpu.make_async_remote_copy(
            src_ref=piece, dst_ref=second.at[i], send_sem=s2.at[i], recv_sem=r2.at[i],
            device_id=(fit, ao_peer(i)), device_id_type=MESH)

    def hop3(i):
        return pltpu.make_async_remote_copy(
            src_ref=both, dst_ref=done.at[i], send_sem=s3.at[i], recv_sem=r3.at[i],
            device_id=(fit_peer(i), ao), device_id_type=MESH)

    def hop_a(c, i):
        return pltpu.make_async_remote_copy(
            src_ref=send.at[c, i], dst_ref=recv.at[c, i], send_sem=sa.at[c, i], recv_sem=ra.at[c, i],
            device_id=(fit, ao_peer(i)), device_id_type=MESH)

    def hop_b(c, i):
        peer = fit_peer(i)
        return pltpu.make_async_remote_copy(
            src_ref=bsend.at[c, peer], dst_ref=brecv.at[c, i], send_sem=sb.at[c, i], recv_sem=rb.at[c, i],
            device_id=(peer, ao), device_id_type=MESH)

    every(1, NF, lambda i: hop1(i).start())
    each(6, 12, turn)

    every(1, NF, lambda i: hop1(i).wait_recv())
    total = own[fit].astype(F32)
    for i in range(1, NF):
        total = total + first[i].astype(F32)
    piece[...] = total.astype(BF16)
    every(1, NA, lambda i: hop2(i).start())

    each(0, NA, look)
    each(12, 22, turn)
    every(1, NA, lambda i: hop2(i).wait_recv())
    for i in range(1, NA):
        total = total + second[i].astype(F32)
    both[...] = total.astype(BF16)
    every(1, NF, lambda i: hop3(i).start())
    coeff[fit] = both[...]
    each(22, 32, turn)
    every(1, NF, lambda i: hop3(i).wait_recv())

    def put(i):
        coeff[lax.rem(fit + NF - i, NF)] = done[i]

    each(1, NF, put)

    pair = coeff[...].reshape(2, W, W)
    orbitals = jnp.concatenate([pair[0], pair[1]], 1)

    def product(v):
        j = lax.div(v, W // WIDE)
        some = pl.ds(pl.multiple_of(lax.rem(v, W // WIDE) * WIDE, WIDE), WIDE)
        r = jnp.dot(flat[j, some].reshape(WIDE * W, W), orbitals, preferred_element_type=F32)
        r = r.astype(BF16)
        half[0, j, some] = r[:, :W].reshape(WIDE, W, W)
        half[1, j, some] = r[:, W:].reshape(WIDE, W, W)

    each(0, MUB * W // WIDE, product)

    def rows_of(first, lo, n):
        return jnp.concatenate(
            [half[h, :, first + v, lo:lo + n, :].reshape(MUB * n, W)
             for h in range(2) for v in range(DEEP)], 1)

    head_row = lax.broadcasted_iota(jnp.int32, (HEAD, W), 0)

    def encode(tile, slot):
        top = jnp.maximum(jnp.max(jnp.abs(tile), axis=0, keepdims=True), 1e-33)
        level = jnp.ceil(jnp.log2(top) * STEP)
        values = jnp.round(tile * (TOP * jnp.exp2(level * (-1.0 / STEP))))
        head = jnp.where(head_row == 0, level.astype(jnp.int32), slot)
        return values.astype(jnp.int32).astype(I16), head.astype(I16)

    def decode_head(head):
        head = head.astype(jnp.int32).astype(F32)
        return jnp.exp2(head[0:1] * (1.0 / STEP)) * (1.0 / TOP), head[1:2]

    def decode(values):
        return values.astype(jnp.int32).astype(F32)

    left = lax.broadcasted_iota(jnp.int32, (CODED, W), 1) < ROWS
    left_row = left[:ROWS]

    def fill(p, i, where_to):
        owner = ao_peer(i)
        one = gram[p, tab[owner * CAP]].astype(jnp.int32)
        two = gram[p, tab[owner * CAP + 1]].astype(jnp.int32)
        where_to[p, i] = jnp.where(left, one, two).astype(I16)

    def store(p, t, tile):
        keep = (screen_ref[t // MUB] * screen_ref[t % MUB]).astype(F32)
        values, head = encode(tile * keep, tile_slot_ref[t])
        gram[p, t, pl.ds(0, ROWS)] = values
        gram[p, t, pl.ds(ROWS, HEAD)] = head

    def share(p):
        gram[p, TILES] = jnp.full((CODED, W), -1, jnp.int32).astype(I16)

        def push(i):
            fill(p, i, send)
            hop_a(p, i).start()

        each(1, NA, push)
        fill(p, 0, recv)

    def block(stage, j, k):
        return acc[stage, j * ROWS:(j + 1) * ROWS, k // 2 * W:(k // 2 + 1) * W]

    for stage, (a, b) in enumerate(((0, 0), (0, 1), (1, 1))):
        acc[stage] = jnp.zeros((MUB * ROWS, MUB * ROWS), F32)

        def deep(i, stage=stage, a=a, b=b):
            one = rows_of(i * DEEP, a * ROWS, ROWS)
            two = one if a == b else rows_of(i * DEEP, b * ROWS, ROWS)
            acc[stage] += lax.dot_general(one, two, NT, preferred_element_type=F32)

        each(0, W // DEEP, deep)
        for j in range(MUB):
            for k in range(MUB):
                tile = block(stage, j, k)
                other = pltpu.roll(tile, ROWS, 1)
                pair = (tile, other) if k % 2 == 0 else (other, tile)
                store(a * 2 + b, j * MUB + k, jnp.where(left_row, pair[0], pair[1]))
        share(a * 2 + b)
        if a != b:
            for k in range(MUB):
                for j in range(0, MUB, 2):
                    tile = block(stage, k, j)
                    turned = jnp.concatenate([tile, tile], 0).T
                    store(2, j * MUB + k, turned[:ROWS])
                    store(2, (j + 1) * MUB + k, turned[ROWS:])
            share(2)

    order = (0, 1, 2, 3)
    for p in order:
        each(1, NA, lambda i, p=p: hop_a(p, i).wait_recv())

        def heads(i, p=p):
            scale, slot = decode_head(recv[p, i, pl.ds(ROWS, HEAD)])
            scales[i] = jnp.broadcast_to(scale, (8, W))
            slots[i] = jnp.broadcast_to(slot, (8, W))

        each(0, NA, heads)

        def band(b, p=p):
            for group in range(0, SLOTS, 8):
                def add(i, sums, group=group):
                    tile = decode(recv[p, i, pl.ds(b * 16, 16)]).reshape(2, 8, W) * scales[i][None]
                    slot = slots[i]
                    return [
                        sums[q] + jnp.where((slot == float(group + q))[None], tile, 0.0)
                        for q in range(8)]

                zero = jnp.zeros((2, 8, W), F32)
                sums = lax.fori_loop(0, NA, add, [zero] * 8, unroll=4)
                for q in range(0, 8, 2):
                    even, odd = sums[q].reshape(16, W), sums[q + 1].reshape(16, W)
                    swapped = pltpu.roll(jnp.where(left[:16], odd, even), ROWS, 1)
                    sums_of[(group + q) // 2, pl.ds(b * 16, 16)] = jnp.where(left[:16], even, odd) + swapped

        each(0, ROWS // 16, band)

        def pack(g, p=p):
            values, head = encode(sums_of[g], jnp.int32(0))
            bsend[p, g, pl.ds(0, ROWS)] = values
            bsend[p, g, pl.ds(ROWS, HEAD)] = head

        each(0, NF, pack)
        each(1, NF, lambda i, p=p: hop_b(p, i).start())
        mine[p] = sums_of[fit]

    every(1, NF, lambda i: hop1(i).wait_send())
    every(1, NA, lambda i: hop2(i).wait_send())
    every(1, NF, lambda i: hop3(i).wait_send())
    for p in order:
        each(1, NA, lambda i, p=p: hop_a(p, i).wait_send())

    def fit_sum(p):
        each(1, NF, lambda i: hop_b(p, i).wait_recv())
        sums = mine[p]
        for i in range(1, NF):
            scale, _ = decode_head(brecv[p, i, pl.ds(ROWS, HEAD)])
            sums = sums + decode(brecv[p, i, pl.ds(0, ROWS)]) * scale
        return sums

    for a in range(2):
        one, two = fit_sum(2 * a), fit_sum(2 * a + 1)
        rows = pl.ds(a * ROWS, ROWS)
        out_ref[0, rows] = jnp.where(left_row, one, pltpu.roll(two, ROWS, 1))
        out_ref[1, rows] = jnp.where(left_row, pltpu.roll(one, ROWS, 1), two)

    for p in order:
        each(1, NF, lambda i, p=p: hop_b(p, i).wait_send())


def on_device(three_index, occ_coeff, occ_owner, screen, tile_owner, tile_slot):
    smem = pl.BlockSpec(memory_space=pltpu.SMEM)
    vmem = pl.BlockSpec(memory_space=pltpu.VMEM)
    dma = pltpu.SemaphoreType.DMA
    part = (PIECE, W)
    return pl.pallas_call(
        whole_kernel,
        out_shape=jax.ShapeDtypeStruct((2, W, W), F32),
        in_specs=[smem, smem, smem, smem, vmem, pl.BlockSpec(memory_space=pl.ANY)],
        out_specs=vmem,
        scratch_shapes=[
            pltpu.VMEM((2, MUB, W, W, W), BF16),
            pltpu.VMEM((MUB, W, W, W), BF16),
            pltpu.VMEM((3, MUB * ROWS, MUB * ROWS), F32),
            pltpu.VMEM((PARTS, TILES + 1, CODED, W), I16),
            pltpu.VMEM((NF,) + part, BF16),
            pltpu.VMEM((NF,) + part, BF16),
            pltpu.VMEM(part, BF16),
            pltpu.VMEM((NA,) + part, BF16),
            pltpu.VMEM(part, BF16),
            pltpu.VMEM((NF,) + part, BF16),
            pltpu.VMEM((NF,) + part, BF16),
            pltpu.VMEM((NA, 8, W), F32),
            pltpu.VMEM((NA, 8, W), F32),
            pltpu.VMEM((PARTS, NA, CODED, W), I16),
            pltpu.VMEM((PARTS, NA, CODED, W), I16),
            pltpu.VMEM((NF, ROWS, W), F32),
            pltpu.VMEM((PARTS, ROWS, W), F32),
            pltpu.VMEM((PARTS, NF, CODED, W), I16),
            pltpu.VMEM((PARTS, NF, CODED, W), I16),
            pltpu.SMEM((NA * CAP,), jnp.int32),
            dma((UNITS,)),
            dma((NF,)), dma((NF,)), dma((NA,)), dma((NA,)), dma((NF,)), dma((NF,)),
            dma((PARTS, NA)), dma((PARTS, NA)), dma((PARTS, NF)), dma((PARTS, NF)),
        ],
        compiler_params=pltpu.CompilerParams(
            collective_id=0, has_side_effects=True, vmem_limit_bytes=63 << 20),
        name="exchange",
    )(occ_owner, screen[:, 0], tile_owner[:, 0], tile_slot, occ_coeff[0], three_index)


def solution(mesh):
    in_specs = (
        P("ao", None, None, "fit"),
        P(("fit", "ao"), None, None),
        P(),
        P("ao", "fit"),
        P(("fit", "ao"), None),
        P(("fit", "ao")),
    )
    out_specs = P(("fit", "ao"), None, None)
    return jax.shard_map(
        on_device, mesh=mesh, in_specs=in_specs, out_specs=out_specs, check_vma=False
    )
```

time: 73 us -> 68.7 us (0.941)
  Pallas kernels: 70.1 us -> 65.9 us
    pallas_call x1, Pallas kernels: 70.1 us -> 65.9 us  [on_device(): pl.pallas_call(whole_kernel, out_shape=jax.ShapeDtypeStruct((2, W, W), F3...]
where the time goes in v4:
time: 68.7 us; the launch traced here: 67.5 us
  Pallas kernels  65.9 us (96%)
  local copies, waits for them, and re-layouts  1.57 us (2%)
    pallas_call x1, Pallas kernels, on_device(): pl.pallas_call(whole_kernel, out_shape=jax.ShapeDtypeStruct((2, W, W), F3...  65.9 us
    unnamed x1, local copies, waits for them, and re-layouts  1.57 us

profile of v4, /device:TPU:0, one launch (start us, length us, event | category | flops | bytes accessed | tf_op | source)
XLA Modules:
  0.0 67.5 jit_solution(14659240746992443155)
XLA Ops:
  0.0 65.9 %exchange.1 = f32[2,128,128]{2,1,0:T(8,128)} custom-call(s32[2]{0:T(128)} %owner_ref.1, s32[4]{0:T(128)} %bitcast.4, s32[16]{0:T(128)} %bitcast.5, s32[16]{0:T(128)} %tile_slot_ref.1, bf16[128,128]{1,0:T(8,128)(2,1)} %bitcast.3, bf16[4,128,128,128]{3,2,1,0:T(8,128)(2,1)} %three_ref.1), custom_call_target="tpu_custom_call" | custom-call | tf_op jit(solution)/shard_map/exchange/pallas_call | solution.py:316
  65.9 1.6 %copy.8 = f32[2,128,128]{2,1,0:T(8,128)} copy(f32[2,128,128]{2,1,0:T(8,128)} %exchange.1) | data formatting | bytes 262144

commit v5 on v4

--- a/solution.py
+++ b/solution.py
@@ -18,9 +18,9 @@
 BANDS = W // BAND
 UNITS = MUB * BANDS
 WIDE = 128
-DEEP = 32
+DEEP = 64
 I16 = jnp.int16
-HEAD = 16
+HEAD = 8
 CODED = ROWS + HEAD
 TOP = 32766.0
 STEP = 16.0
@@ -41,10 +41,11 @@
 
 
 def whole_kernel(
-    owner_ref, screen_ref, tile_owner_ref, tile_slot_ref, occ_ref, three_ref, out_ref,
+    owner_in, screen_in, tile_owner_in, tile_slot_in, occ_in, three_ref, out_hbm,
+    out_ref, owner_ref, screen_ref, tile_owner_ref, tile_slot_ref, occ_ref,
     half, flat, acc, gram, own, first, piece, second, both, done, coeff,
-    scales, slots, send, recv, sums_of, mine, bsend, brecv, tab,
-    load, s1, r1, s2, r2, s3, r3, sa, ra, sb, rb,
+    scales, slots, send, recv, sums_of, mine, sides, bsend, brecv, tab,
+    load, small, s1, r1, s2, r2, s3, r3, sa, ra, sb, rb,
 ):
     fit, ao = lax.axis_index("fit"), lax.axis_index("ao")
     me = fit * NA + ao
@@ -62,6 +63,13 @@
         rows = pl.ds(pl.multiple_of(b * BAND, BAND), BAND)
         return pltpu.make_async_copy(three_ref.at[j, :, rows], half.at[1, j, :, rows], load.at[u])
 
+    smalls = [
+        pltpu.make_async_copy(here, there, small.at[n])
+        for n, (here, there) in enumerate((
+            (owner_in, owner_ref), (occ_in, occ_ref), (tile_owner_in, tile_owner_ref),
+            (tile_slot_in, tile_slot_ref), (screen_in, screen_ref)))]
+    for copy in smalls:
+        copy.start()
     each(0, UNITS, lambda u: fetch(u).start())
 
     barrier = pltpu.get_barrier_semaphore()
@@ -75,6 +83,8 @@
     every(1, NF, greet_fit)
     every(1, NA, greet_ao)
 
+    for copy in smalls:
+        copy.wait()
     occ = occ_ref[...].astype(F32)
     for which in range(2):
         keep = jnp.where(owner_ref[which] == me, 1.0, 0.0).astype(F32)
@@ -195,12 +205,13 @@
 
     left = lax.broadcasted_iota(jnp.int32, (CODED, W), 1) < ROWS
     left_row = left[:ROWS]
+    sides[0] = jnp.where(left, -1, 0).astype(I16)
+    sides[1] = jnp.where(left, 0, -1).astype(I16)
 
     def fill(p, i, where_to):
         owner = ao_peer(i)
-        one = gram[p, tab[owner * CAP]].astype(jnp.int32)
-        two = gram[p, tab[owner * CAP + 1]].astype(jnp.int32)
-        where_to[p, i] = jnp.where(left, one, two).astype(I16)
+        one, two = gram[p, tab[owner * CAP]], gram[p, tab[owner * CAP + 1]]
+        where_to[p, i] = (one & sides[0]) | (two & sides[1])
 
     def store(p, t, tile):
         keep = (screen_ref[t // MUB] * screen_ref[t % MUB]).astype(F32)
@@ -267,7 +278,7 @@
                         for q in range(8)]
 
                 zero = jnp.zeros((2, 8, W), F32)
-                sums = lax.fori_loop(0, NA, add, [zero] * 8, unroll=4)
+                sums = lax.fori_loop(0, NA, add, [zero] * 8, unroll=16)
                 for q in range(0, 8, 2):
                     even, odd = sums[q].reshape(16, W), sums[q + 1].reshape(16, W)
                     swapped = pltpu.roll(jnp.where(left[:16], odd, even), ROWS, 1)
@@ -298,27 +309,38 @@
             sums = sums + decode(brecv[p, i, pl.ds(0, ROWS)]) * scale
         return sums
 
+    def leave(a):
+        rows = pl.ds(a * ROWS, ROWS)
+        return pltpu.make_async_copy(out_ref.at[:, rows], out_hbm.at[:, rows], small.at[a])
+
     for a in range(2):
         one, two = fit_sum(2 * a), fit_sum(2 * a + 1)
         rows = pl.ds(a * ROWS, ROWS)
         out_ref[0, rows] = jnp.where(left_row, one, pltpu.roll(two, ROWS, 1))
         out_ref[1, rows] = jnp.where(left_row, pltpu.roll(one, ROWS, 1), two)
+        leave(a).start()
 
     for p in order:
         each(1, NF, lambda i, p=p: hop_b(p, i).wait_send())
+    for a in range(2):
+        leave(a).wait()
 
 
 def on_device(three_index, occ_coeff, occ_owner, screen, tile_owner, tile_slot):
-    smem = pl.BlockSpec(memory_space=pltpu.SMEM)
-    vmem = pl.BlockSpec(memory_space=pltpu.VMEM)
     dma = pltpu.SemaphoreType.DMA
     part = (PIECE, W)
     return pl.pallas_call(
         whole_kernel,
         out_shape=jax.ShapeDtypeStruct((2, W, W), F32),
-        in_specs=[smem, smem, smem, smem, vmem, pl.BlockSpec(memory_space=pl.ANY)],
-        out_specs=vmem,
+        in_specs=[pl.BlockSpec(memory_space=pl.ANY)] * 6,
+        out_specs=pl.BlockSpec(memory_space=pl.ANY),
         scratch_shapes=[
+            pltpu.VMEM((2, W, W), F32),
+            pltpu.SMEM((2,), jnp.int32),
+            pltpu.SMEM((MUB,), jnp.int32),
+            pltpu.SMEM((TILES,), jnp.int32),
+            pltpu.SMEM((TILES,), jnp.int32),
+            pltpu.VMEM((W, W), BF16),
             pltpu.VMEM((2, MUB, W, W, W), BF16),
             pltpu.VMEM((MUB, W, W, W), BF16),
             pltpu.VMEM((3, MUB * ROWS, MUB * ROWS), F32),
@@ -336,10 +358,11 @@
             pltpu.VMEM((PARTS, NA, CODED, W), I16),
             pltpu.VMEM((NF, ROWS, W), F32),
             pltpu.VMEM((PARTS, ROWS, W), F32),
+            pltpu.VMEM((2, CODED, W), I16),
             pltpu.VMEM((PARTS, NF, CODED, W), I16),
             pltpu.VMEM((PARTS, NF, CODED, W), I16),
             pltpu.SMEM((NA * CAP,), jnp.int32),
-            dma((UNITS,)),
+            dma((UNITS,)), dma((5,)),
             dma((NF,)), dma((NF,)), dma((NA,)), dma((NA,)), dma((NF,)), dma((NF,)),
             dma((PARTS, NA)), dma((PARTS, NA)), dma((PARTS, NF)), dma((PARTS, NF)),
         ],

time: 68.7 us -> 65.6 us (0.955)
  Pallas kernels: 65.9 us -> 62.9 us
    pallas_call x1, Pallas kernels: 65.9 us -> 62.9 us  [on_device(): pl.pallas_call(whole_kernel, out_shape=jax.ShapeDtypeStruct((2, W, W), F3...]
where the time goes in v5:
time: 65.6 us; the launch traced here: 64.5 us
  Pallas kernels  62.9 us (96%)
  local copies, waits for them, and re-layouts  1.57 us (2%)
    pallas_call x1, Pallas kernels, on_device(): pl.pallas_call(whole_kernel, out_shape=jax.ShapeDtypeStruct((2, W, W), F3...  62.9 us
    unnamed x1, local copies, waits for them, and re-layouts  1.57 us

profile of v5, /device:TPU:0, one launch (start us, length us, event | category | flops | bytes accessed | tf_op | source)
XLA Modules:
  0.0 64.5 jit_solution(14332284553460491666)
XLA Ops:
  0.0 62.9 %exchange.1 = f32[2,128,128]{2,1,0:T(8,128)} custom-call(s32[2]{0:T(128)} %owner_in.1, s32[4]{0:T(128)} %bitcast.4, s32[16]{0:T(128)} %bitcast.5, s32[16]{0:T(128)} %tile_slot_in.1, bf16[128,128]{1,0:T(8,128)(2,1)} %bitcast.3, bf16[4,128,128,128]{3,2,1,0:T(8,128)(2,1)} %three_ref.1), custom_call_target="tpu_custom_call" | custom-call | tf_op jit(solution)/shard_map/exchange/pallas_call | solution.py:332
  62.9 1.6 %copy.8 = f32[2,128,128]{2,1,0:T(8,128)} copy(f32[2,128,128]{2,1,0:T(8,128)} %exchange.1) | data formatting | bytes 262144

commit v6 on v5

--- a/solution.py
+++ b/solution.py
@@ -99,7 +99,7 @@
                 tile[r] = jnp.where(jnp.logical_and(hit, count == r), t, tile[r])
             count = count + jnp.where(hit, 1, 0)
         for r in range(CAP):
-            tab[owner * CAP + r] = tile[r]
+            tab[owner * CAP + r] = tile[r] if r == 0 else tile[r] + 1 - 2 * lax.rem(tile[r], 2)
 
     def turn(u):
         fetch(u).wait()
@@ -189,12 +189,13 @@
 
     head_row = lax.broadcasted_iota(jnp.int32, (HEAD, W), 0)
 
-    def encode(tile, slot):
+    def coded(tile):
         top = jnp.maximum(jnp.max(jnp.abs(tile), axis=0, keepdims=True), 1e-33)
         level = jnp.ceil(jnp.log2(top) * STEP)
-        values = jnp.round(tile * (TOP * jnp.exp2(level * (-1.0 / STEP))))
-        head = jnp.where(head_row == 0, level.astype(jnp.int32), slot)
-        return values.astype(jnp.int32).astype(I16), head.astype(I16)
+        return jnp.round(tile * (TOP * jnp.exp2(level * (-1.0 / STEP)))), level.astype(jnp.int32)
+
+    def narrow(values):
+        return values.astype(jnp.int32).astype(I16)
 
     def decode_head(head):
         head = head.astype(jnp.int32).astype(F32)
@@ -213,14 +214,21 @@
         one, two = gram[p, tab[owner * CAP]], gram[p, tab[owner * CAP + 1]]
         where_to[p, i] = (one & sides[0]) | (two & sides[1])
 
-    def store(p, t, tile):
-        keep = (screen_ref[t // MUB] * screen_ref[t % MUB]).astype(F32)
-        values, head = encode(tile * keep, tile_slot_ref[t])
-        gram[p, t, pl.ds(0, ROWS)] = values
-        gram[p, t, pl.ds(ROWS, HEAD)] = head
+    def store(p, t, tiles):
+        keep = [
+            jnp.full((1, W), (screen_ref[t // MUB] * screen_ref[n % MUB]).astype(F32), F32)
+            for n in (t, t + 1)]
+        values, level = coded(tiles * jnp.where(left_row[:1], keep[0], keep[1]))
+        slot = jnp.where(left[:HEAD], tile_slot_ref[t], tile_slot_ref[t + 1])
+        head = jnp.where(head_row == 0, level, slot)
+        gram[p, t, pl.ds(0, ROWS)] = narrow(values)
+        gram[p, t, pl.ds(ROWS, HEAD)] = head.astype(I16)
+        gram[p, t + 1, pl.ds(0, ROWS)] = narrow(pltpu.roll(values, ROWS, 1))
+        gram[p, t + 1, pl.ds(ROWS, HEAD)] = pltpu.roll(head, ROWS, 1).astype(I16)
 
     def share(p):
-        gram[p, TILES] = jnp.full((CODED, W), -1, jnp.int32).astype(I16)
+        for t in range(TILES, TILES + 2):
+            gram[p, t] = jnp.full((CODED, W), -1, jnp.int32).astype(I16)
 
         def push(i):
             fill(p, i, send)
@@ -242,31 +250,30 @@
 
         each(0, W // DEEP, deep)
         for j in range(MUB):
-            for k in range(MUB):
-                tile = block(stage, j, k)
-                other = pltpu.roll(tile, ROWS, 1)
-                pair = (tile, other) if k % 2 == 0 else (other, tile)
-                store(a * 2 + b, j * MUB + k, jnp.where(left_row, pair[0], pair[1]))
+            for k in range(0, MUB, 2):
+                store(a * 2 + b, j * MUB + k, block(stage, j, k))
         share(a * 2 + b)
         if a != b:
-            for k in range(MUB):
+            for k in range(0, MUB, 2):
                 for j in range(0, MUB, 2):
-                    tile = block(stage, k, j)
-                    turned = jnp.concatenate([tile, tile], 0).T
+                    turned = jnp.concatenate([block(stage, k, j), block(stage, k + 1, j)], 0).T
                     store(2, j * MUB + k, turned[:ROWS])
                     store(2, (j + 1) * MUB + k, turned[ROWS:])
             share(2)
 
     order = (0, 1, 2, 3)
     for p in order:
-        each(1, NA, lambda i, p=p: hop_a(p, i).wait_recv())
-
         def heads(i, p=p):
             scale, slot = decode_head(recv[p, i, pl.ds(ROWS, HEAD)])
             scales[i] = jnp.broadcast_to(scale, (8, W))
             slots[i] = jnp.broadcast_to(slot, (8, W))
 
-        each(0, NA, heads)
+        def arrive(i, p=p, heads=heads):
+            hop_a(p, i).wait_recv()
+            heads(i)
+
+        heads(0)
+        each(1, NA, arrive)
 
         def band(b, p=p):
             for group in range(0, SLOTS, 8):
@@ -286,13 +293,14 @@
 
         each(0, ROWS // 16, band)
 
-        def pack(g, p=p):
-            values, head = encode(sums_of[g], jnp.int32(0))
-            bsend[p, g, pl.ds(0, ROWS)] = values
-            bsend[p, g, pl.ds(ROWS, HEAD)] = head
-
-        each(0, NF, pack)
-        each(1, NF, lambda i, p=p: hop_b(p, i).start())
+        def pack(i, p=p):
+            g = fit_peer(i)
+            values, level = coded(sums_of[g])
+            bsend[p, g, pl.ds(0, ROWS)] = narrow(values)
+            bsend[p, g, pl.ds(ROWS, HEAD)] = jnp.where(head_row == 0, level, 0).astype(I16)
+            hop_b(p, i).start()
+
+        each(1, NF, pack)
         mine[p] = sums_of[fit]
 
     every(1, NF, lambda i: hop1(i).wait_send())
@@ -344,7 +352,7 @@
             pltpu.VMEM((2, MUB, W, W, W), BF16),
             pltpu.VMEM((MUB, W, W, W), BF16),
             pltpu.VMEM((3, MUB * ROWS, MUB * ROWS), F32),
-            pltpu.VMEM((PARTS, TILES + 1, CODED, W), I16),
+            pltpu.VMEM((PARTS, TILES + 2, CODED, W), I16),
             pltpu.VMEM((NF,) + part, BF16),
             pltpu.VMEM((NF,) + part, BF16),
             pltpu.VMEM(part, BF16),

time: 65.6 us -> 65.1 us (level)
  no operation moved by 1% of the time
where the time goes in v6:
time: 65.1 us; the launch traced here: 64 us
  Pallas kernels  62.4 us (96%)
  local copies, waits for them, and re-layouts  1.57 us (2%)
    pallas_call x1, Pallas kernels, on_device(): pl.pallas_call(whole_kernel, out_shape=jax.ShapeDtypeStruct((2, W, W), F3...  62.4 us
    unnamed x1, local copies, waits for them, and re-layouts  1.57 us

profile of v6, /device:TPU:0, one launch (start us, length us, event | category | flops | bytes accessed | tf_op | source)
XLA Modules:
  0.0 64.0 jit_solution(3880097231504461898)
XLA Ops:
  0.0 62.4 %exchange.1 = f32[2,128,128]{2,1,0:T(8,128)} custom-call(s32[2]{0:T(128)} %owner_in.1, s32[4]{0:T(128)} %bitcast.4, s32[16]{0:T(128)} %bitcast.5, s32[16]{0:T(128)} %tile_slot_in.1, bf16[128,128]{1,0:T(8,128)(2,1)} %bitcast.3, bf16[4,128,128,128]{3,2,1,0:T(8,128)(2,1)} %three_ref.1), custom_call_target="tpu_custom_call" | custom-call | tf_op jit(solution)/shard_map/exchange/pallas_call | solution.py:340
  62.4 1.6 %copy.8 = f32[2,128,128]{2,1,0:T(8,128)} copy(f32[2,128,128]{2,1,0:T(8,128)} %exchange.1) | data formatting | bytes 262144

commit v7 on v6

--- a/solution.py
+++ b/solution.py
@@ -151,7 +151,7 @@
     for i in range(1, NF):
         total = total + first[i].astype(F32)
     piece[...] = total.astype(BF16)
-    every(1, NA, lambda i: hop2(i).start())
+    every(1, NA, lambda n: hop2(NA - n).start())
 
     each(0, NA, look)
     each(12, 22, turn)
@@ -230,7 +230,8 @@
         for t in range(TILES, TILES + 2):
             gram[p, t] = jnp.full((CODED, W), -1, jnp.int32).astype(I16)
 
-        def push(i):
+        def push(n):
+            i = NA - n
             fill(p, i, send)
             hop_a(p, i).start()
 

time: 65.1 us -> 65.3 us (level)
  no operation moved by 1% of the time
where the time goes in v7:
time: 65.3 us; the launch traced here: 64.1 us
  Pallas kernels  62.5 us (96%)
  local copies, waits for them, and re-layouts  1.57 us (2%)
    pallas_call x1, Pallas kernels, on_device(): pl.pallas_call(whole_kernel, out_shape=jax.ShapeDtypeStruct((2, W, W), F3...  62.5 us
    unnamed x1, local copies, waits for them, and re-layouts  1.57 us

profile of v7, /device:TPU:0, one launch (start us, length us, event | category | flops | bytes accessed | tf_op | source)
XLA Modules:
  0.0 64.1 jit_solution(12590089472574812529)
XLA Ops:
  0.0 62.5 %exchange.1 = f32[2,128,128]{2,1,0:T(8,128)} custom-call(s32[2]{0:T(128)} %owner_in.1, s32[4]{0:T(128)} %bitcast.4, s32[16]{0:T(128)} %bitcast.5, s32[16]{0:T(128)} %tile_slot_in.1, bf16[128,128]{1,0:T(8,128)(2,1)} %bitcast.3, bf16[4,128,128,128]{3,2,1,0:T(8,128)(2,1)} %three_ref.1), custom_call_target="tpu_custom_call" | custom-call | tf_op jit(solution)/shard_map/exchange/pallas_call | solution.py:341
  62.6 1.6 %copy.8 = f32[2,128,128]{2,1,0:T(8,128)} copy(f32[2,128,128]{2,1,0:T(8,128)} %exchange.1) | data formatting | bytes 262144

commit v8 on v7

--- a/solution.py
+++ b/solution.py
@@ -13,6 +13,7 @@
 ORB = 2 * W
 PIECE = W // 4
 PARTS = 4
+FAR_FIRST = (4, 3, 5, 2, 6, 1, 7)
 ROWS = W // 2
 BAND = 16
 BANDS = W // BAND
@@ -143,7 +144,8 @@
             src_ref=bsend.at[c, peer], dst_ref=brecv.at[c, i], send_sem=sb.at[c, i], recv_sem=rb.at[c, i],
             device_id=(peer, ao), device_id_type=MESH)
 
-    every(1, NF, lambda i: hop1(i).start())
+    for i in FAR_FIRST:
+        hop1(i).start()
     each(6, 12, turn)
 
     every(1, NF, lambda i: hop1(i).wait_recv())
@@ -159,7 +161,8 @@
     for i in range(1, NA):
         total = total + second[i].astype(F32)
     both[...] = total.astype(BF16)
-    every(1, NF, lambda i: hop3(i).start())
+    for i in FAR_FIRST:
+        hop3(i).start()
     coeff[fit] = both[...]
     each(22, 32, turn)
     every(1, NF, lambda i: hop3(i).wait_recv())

time: 65.3 us -> 65.2 us (level)
  no operation moved by 1% of the time
where the time goes in v8:
time: 65.2 us; the launch traced here: 64.1 us
  Pallas kernels  62.5 us (96%)
  local copies, waits for them, and re-layouts  1.57 us (2%)
    pallas_call x1, Pallas kernels, on_device(): pl.pallas_call(whole_kernel, out_shape=jax.ShapeDtypeStruct((2, W, W), F3...  62.5 us
    unnamed x1, local copies, waits for them, and re-layouts  1.57 us

profile of v8, /device:TPU:0, one launch (start us, length us, event | category | flops | bytes accessed | tf_op | source)
XLA Modules:
  0.0 64.1 jit_solution(11573383511701019346)
XLA Ops:
  0.0 62.5 %exchange.1 = f32[2,128,128]{2,1,0:T(8,128)} custom-call(s32[2]{0:T(128)} %owner_in.1, s32[4]{0:T(128)} %bitcast.4, s32[16]{0:T(128)} %bitcast.5, s32[16]{0:T(128)} %tile_slot_in.1, bf16[128,128]{1,0:T(8,128)(2,1)} %bitcast.3, bf16[4,128,128,128]{3,2,1,0:T(8,128)(2,1)} %three_ref.1), custom_call_target="tpu_custom_call" | custom-call | tf_op jit(solution)/shard_map/exchange/pallas_call | solution.py:344
  62.5 1.6 %copy.8 = f32[2,128,128]{2,1,0:T(8,128)} copy(f32[2,128,128]{2,1,0:T(8,128)} %exchange.1) | data formatting | bytes 262144
